TPU v7x, 1024 devices: a whole 4x8x16 slice. The times are simulated.
1024 devices in a mesh: group: 8 (over y_lo, x), member: 128 (over z, y_hi, core).
Axes of the slice: x: 4, y: 8 (y_hi: 4, y_lo: 2; y = y_hi * 2 + y_lo), z: 16, core: 2. Of those that a mesh axis runs over, the one named last changes fastest.
Arguments:
- points: bfloat16 [262144, 768], P(('group', 'member')), may hold values from -9 to 9
- centroids: bfloat16 [16384, 768], P('group'), may hold values from -5 to 5
- dest_group: int32 [262144, 1], P(('group', 'member')), may hold values from 0 to 7; in each aligned block of 256 rows (0 to 255, 256 to 511, ...) at most 64 rows name the same one
Outputs:
- refined: bfloat16 [16384, 768], P(('group', 'member'))
Inputs may be any that keep to these rules, and one draw needn't show every extreme that they name: `dest_group`: among the 256 rows of one device, at most 64 name the same group, a bound that some block reaches of them.
All inputs are finite; a program needn't handle non-finite values.
Results may differ from a plain program's by a relative error of at most 0.0025.
Values may be sent and summed in bfloat16 or wider, within the bound.
A program may use at most 64 MiB of HBM per device.

v0:
```python
import jax
import jax.numpy as jnp
from jax import lax
from jax.sharding import Mesh
from jax.sharding import PartitionSpec as P

MEMBER = ("member_0", "member_1", "member_2")
GROUP_MEMBER = ("group", "member_0", "member_1", "member_2")


score_scale = 0.15


def in_one_piece(arrays, axis, split_dim, concat_dim, along):
    both = jnp.concatenate(arrays, axis=along)
    out, at, done = (
        lax.all_to_all(both, axis, split_axis=split_dim, concat_axis=concat_dim, tiled=True),
        0,
        [],
    )
    for a in arrays:
        done.append(lax.slice_in_dim(out, at, at + a.shape[along], axis=along))
        at += a.shape[along]
    return tuple(done)


def sum_in_order(pieces, axes, turns):
    inside = pieces.shape[1:]
    pieces = pieces.reshape(*(lax.axis_size(a) for a in axes), *inside)
    pieces = jnp.moveaxis(pieces, turns, range(len(axes))).reshape(-1, *inside)
    for k in turns:
        pieces = lax.psum_scatter(pieces, axes[k], scatter_dimension=0, tiled=True)
    return pieces[0]


def in_blocks(shard, dim, peers):
    lengths = shard.shape
    pieces = shard.reshape(*lengths[:dim], peers, lengths[dim] // peers, *lengths[dim + 1 :])
    return jnp.moveaxis(pieces, dim, 0)


def summed_rows(shard, axes, turns, dim):
    peers = lax.axis_size(axes)
    return sum_in_order(in_blocks(shard, dim, peers), axes, turns)


def local(points, centroids, dest_group):
    group_count = lax.axis_size("group")
    member_count = lax.axis_size(MEMBER)
    point_rows = points.shape[0]
    capacity = point_rows // 4
    feature_dim = points.shape[1]
    fine_count = centroids.shape[0]
    destination = dest_group[:, 0]
    in_group = (destination[:, None] == jnp.arange(group_count, dtype=jnp.int32)[None, :]).astype(
        jnp.int32
    )
    earlier = jnp.cumsum(in_group, axis=0) - in_group
    own_rank = jnp.sum(earlier * in_group, axis=1)
    slot_index = destination * capacity + own_rank
    placement = (
        jnp.arange(group_count * capacity, dtype=jnp.int32)[:, None] == slot_index[None, :]
    ).astype(jnp.bfloat16)
    packed = jnp.dot(placement, points, preferred_element_type=jnp.float32).astype(jnp.bfloat16)
    packed = packed.reshape(group_count, capacity, feature_dim)
    slot_flags = jnp.dot(
        placement, jnp.ones((point_rows, 1), jnp.bfloat16), preferred_element_type=jnp.float32
    )
    slot_flags = slot_flags.astype(jnp.bfloat16).reshape(group_count, capacity, 1)
    centroid_f = centroids.astype(jnp.float32)
    centroid_norms = jnp.sum(centroid_f * centroid_f, axis=1)
    arrived, marks = in_one_piece((packed, slot_flags), "group", 0, 0, 2)
    rows = arrived.reshape(-1, feature_dim)
    scores = score_scale * (
        jnp.dot(rows, centroids.T, preferred_element_type=jnp.float32)
        - 0.5 * centroid_norms[None, :]
    )
    weights = jax.nn.softmax(scores, axis=-1) * marks.reshape(-1, 1).astype(jnp.float32)
    responsibility = weights.astype(jnp.bfloat16).reshape(
        arrived.shape[0], arrived.shape[1], fine_count
    )
    all_rows = arrived.reshape(-1, feature_dim)
    all_weights = responsibility.reshape(-1, fine_count)
    weighted = jnp.dot(all_weights.T, all_rows, preferred_element_type=jnp.float32)
    soft_counts = jnp.dot(
        jnp.ones((1, all_weights.shape[0]), jnp.bfloat16),
        all_weights,
        preferred_element_type=jnp.float32,
    )[0]
    member_index = lax.axis_index(MEMBER)
    tile_sums, tile_counts = (
        summed_rows(weighted, MEMBER, (2, 0, 1), 0),
        summed_rows(soft_counts, MEMBER, (2, 0, 1), 0),
    )
    tile_rows = fine_count // member_count
    old_tile = lax.dynamic_slice_in_dim(centroid_f, member_index * tile_rows, tile_rows, 0)
    refined = ((tile_sums + old_tile) / (tile_counts + 1.0)[:, None]).astype(jnp.bfloat16)
    return refined


def solution(mesh):
    finer = Mesh(
        mesh.devices.reshape(mesh.shape["group"], 16, 4, 2),
        ("group", "member_0", "member_1", "member_2"),
    )
    placed = (P(GROUP_MEMBER, None), P("group", None), P(GROUP_MEMBER, None))
    return jax.shard_map(
        local, mesh=finer, in_specs=placed, out_specs=P(GROUP_MEMBER, None), check_vma=False
    )
```

profile of v0, /device:TPU:4, one launch (start us, length us, event | category | flops | bytes accessed | tf_op | source)
XLA Modules:
  0.0 268.4 jit_solution(15656254188808709685)
XLA Ops:
  6.5 0.8 fusion.10
  8.2 0.8 fusion.9
  9.9 0.9 reshape.84
  11.2 1.9 pad_maximum_fusion
  13.1 17.2 %all-to-all-start = ((bf16[8,64,769]{2,1,0:T(8,128)(2,1)}), bf16[8,64,769]{2,1,0:T(8,128)(2,1)}, u32[]{:S(2)}, u32[]{:S(2)}) async-start(bf16[8,64,769]{2,1,0:T(8,128)(2,1)} %pad_maximum_fusion), calls=%async_computation | async-start | bytes 1835008 | tf_op jit(solution)/shard_map/all_to_all | solution.py:17
  31.1 7.6 %all-to-all-done = bf16[8,64,769]{2,1,0:T(8,128)(2,1)} async-done(((bf16[8,64,769]{2,1,0:T(8,128)(2,1)}), bf16[8,64,769]{2,1,0:T(8,128)(2,1)}, u32[]{:S(2)}, u32[]{:S(2)}) %all-to-all-start) | async-done | bytes 787488 | tf_op jit(solution)/shard_map/all_to_all | solution.py:17
  38.7 1.0 convert_reduce_fusion
  39.8 1.2 slice.17
  41.0 1.9 fusion
  43.0 0.9 fusion.1
  43.9 2.3 fusion.2
  46.3 2.9 %copy.10 = bf16[2048,512]{1,0:T(8,128)(2,1)S(1)} copy(bf16[2048,512]{0,1:T(8,128)(2,1)} %fusion.2) | data formatting | bytes 4194304 | tf_op jit(solution)/shard_map/convert_element_type | solution.py:79
  49.2 1.8 convolution_bitcast_fusion
  51.0 3.2 %copy.11 = f32[2,16,4,16,768]{4,3,2,1,0:T(8,128)} copy(f32[2,16,4,16,768]{4,3,0,2,1:T(8,128)S(1)} %convolution_bitcast_fusion) | data formatting | bytes 12582912 | tf_op jit(solution)/shard_map/transpose | solution.py:30
  54.3 27.3 %reduce-scatter.5.cloned.1.call-done = f32[64,16,768]{2,1,0:T(8,128)} async-done(((f32[128,16,768]{2,1,0:T(8,128)}), f32[64,16,768]{2,1,0:T(8,128)}) %reduce-scatter.5.cloned.1.call-update) | async-done | bytes 3145744 | tf_op jit(solution)/shard_map/reduce_scatter | solution.py:32
  81.7 2.5 fusion.11
  84.9 83.1 %reduce-scatter.7.cloned.1.call-done = f32[4,16,768]{2,1,0:T(8,128)} async-done(((f32[64,16,768]{2,1,0:T(8,128)}), f32[4,16,768]{2,1,0:T(8,128)}) %reduce-scatter.7.cloned.1.call-update) | async-done | bytes 196624 | tf_op jit(solution)/shard_map/reduce_scatter | solution.py:32
  168.0 5.0 %convert_element_type.40 = f32[2048,768]{1,0:T(8,128)} convert(bf16[2048,768]{1,0:T(8,128)(2,1)} %param.4) | non-fusion elementwise | flops 1572864 | bytes 9437184 | tf_op jit(solution)/shard_map/convert_element_type | solution.py:70
  173.1 1.3 dynamic-slice.2
  174.4 1.3 dynamic-slice
  176.3 12.6 %reduce-scatter.11.cloned.1.call-done = f32[64,16]{1,0:T(8,128)} async-done(((f32[128,16]{1,0:T(8,128)}), f32[64,16]{1,0:T(8,128)}) %reduce-scatter.11.cloned.1.call-update) | async-done | bytes 4112 | tf_op jit(solution)/shard_map/reduce_scatter | solution.py:32
  188.9 58.5 %all-reduce = f32[64,16]{1,0:T(8,128)S(1)} all-reduce(f32[64,16]{1,0:T(8,128)} %reduce-scatter.11.cloned.1.call-done), channel_id=6, replica_groups=mesh['group'=8,'member_0'=16,'member_1'=4,'member_2'=2] {'member_0'}, use_global_device_ids=true, to_apply=%region_10.11.clone | all-reduce | flops 1024 | bytes 8192
  247.4 12.3 %all-reduce.1 = f32[4,16]{1,0:T(4,128)S(1)} all-reduce(f32[4,16]{1,0:T(4,128)S(1)} %constant_dynamic-slice_fusion.1), channel_id=7, replica_groups=mesh['group'=8,'member_0'=16,'member_1'=4,'member_2'=2] {'member_1'}, use_global_device_ids=true, to_apply=%region_11.12.clone | all-reduce | flops 64 | bytes 512
  260.3 1.5 fusion.7
  (31 shorter events, 4.4 us)
Async XLA Ops:
  6.5 4.3 %copy-start = (bf16[256,768]{1,0:T(8,128)(2,1)S(1)}, bf16[256,768]{1,0:T(8,128)(2,1)}, u32[]{:S(2)}) copy-start(bf16[256,768]{1,0:T(8,128)(2,1)} %param.3) | copy-start | bytes 1179652
  6.5 23.8 %copy-start.1 = (bf16[2048,768]{1,0:T(8,128)(2,1)S(1)}, bf16[2048,768]{1,0:T(8,128)(2,1)}, u32[]{:S(2)}) copy-start(bf16[2048,768]{1,0:T(8,128)(2,1)} %param.4) | copy-start | bytes 9437188
  13.1 25.6 %all-to-all-start = ((bf16[8,64,769]{2,1,0:T(8,128)(2,1)}), bf16[8,64,769]{2,1,0:T(8,128)(2,1)}, u32[]{:S(2)}, u32[]{:S(2)}) async-start(bf16[8,64,769]{2,1,0:T(8,128)(2,1)} %pad_maximum_fusion), calls=%async_computation | async-start | bytes 1835008 | tf_op jit(solution)/shard_map/all_to_all | solution.py:17
  30.4 51.2 %reduce-scatter.5.cloned.1.call-start = ((), (), s32[]{:S(2)}) async-start(), calls=%async_computation.5 | async-start | bytes 9437184 | tf_op jit(solution)/shard_map/reduce_scatter | solution.py:32
  41.0 2.0 copy-start.2
  43.9 5.2 %copy-start.3 = (bf16[8,64,768]{2,1,0:T(8,128)(2,1)S(1)}, bf16[8,64,768]{2,1,0:T(8,128)(2,1)}, u32[]{:S(2)}) copy-start(bf16[8,64,768]{2,1,0:T(8,128)(2,1)} %copy-done.2) | copy-start | bytes 2359300
  54.2 113.8 %reduce-scatter.7.cloned.1.call-start = ((), (), s32[]{:S(2)}) async-start(), calls=%async_computation.6 | async-start | bytes 3342336 | tf_op jit(solution)/shard_map/reduce_scatter | solution.py:32
  81.6 107.3 %reduce-scatter.11.cloned.1.call-start = ((), (), s32[]{:S(2)}) async-start(), calls=%async_computation.8 | async-start | bytes 98304 | tf_op jit(solution)/shard_map/reduce_scatter | solution.py:32
  84.9 175.5 %reduce-scatter.9.cloned.1.call-start = ((), (), s32[]{:S(2)}) async-start(), calls=%async_computation.7 | async-start | bytes 245760 | tf_op jit(solution)/shard_map/reduce_scatter | solution.py:32
Sparse Core Ops, SparseCore 0:
  54.3 27.2 reduce-scatter.4
  85.0 82.9 reduce-scatter.6
  171.3 17.5 reduce-scatter.10
  192.1 34.8 reduce-scatter.8
where the time goes:
time: 269 us; the launch traced here: 268 us
  waiting for transfers between devices  131 us (49%)
  blocking collectives  70.8 us (26%)
  starting transfers between devices  17.4 us (6%)
  other arithmetic  17 us (6%)
  between operations  13.9 us (5%)
  local copies, waits for them, and re-layouts  11.8 us (4%)
  matrix products  6.85 us (3%)
    reduce_scatter x4, waiting for transfers between devices, sum_in_order(): pieces = lax.psum_scatter(pieces, axes[k], scatter_dimension=0, tiled=True)  123 us
    unnamed x2, blocking collectives  70.8 us
    all_to_all x1, starting transfers between devices, in_one_piece(): lax.all_to_all(both, axis, split_axis=split_dim, concat_axis=concat_dim,...  17.2 us
    all_to_all x1, waiting for transfers between devices, in_one_piece(): lax.all_to_all(both, axis, split_axis=split_dim, concat_axis=concat_dim,...  7.64 us
  transfers between devices with their start and end apart: 5, of which 4 were waited for; matrix products, arithmetic and copies ran while one was open for 5% of the time, Pallas kernels for 0%

commit v1 on v0

v1 whole, which is shorter than its diff:
```python
import functools

import jax
import jax.numpy as jnp
from jax import lax
from jax.experimental import pallas as pl
from jax.experimental.pallas import tpu as pltpu
from jax.sharding import PartitionSpec as P

MESH = pl.DeviceIdType.MESH
SCALE = 0.15
UNUSED = 64.0
CORES = 2
HIGH_Y = 4
F32, BF16, I32 = jnp.float32, jnp.bfloat16, jnp.int32
NT = (((1,), (1,)), ((), ()))


def iota(shape, dim):
    return lax.broadcasted_iota(I32, shape, dim)


def refit(
    groups, depth, wide, batch,
    points, table, dest, out,
    rows_in, packed, rows, cents, half_norms, scores, weights, sums, counts,
    stats, other_stats, z_out, z_in, zc_out, zc_in, total, y_out, y_in, yc_out, yc_in,
    load_sem, table_sem, a_send, a_recv, f_send, f_recv, s_send, s_recv,
    z_send, z_recv, zc_send, zc_recv, y_send, y_recv, yc_send, yc_recv,
):
    count, width = points.shape
    capacity = packed.shape[1]
    piece = cents.shape[2]
    chunk = wide * piece
    half_depth = depth // 2
    along_x = groups // 2
    block = along_x * capacity

    g, me = lax.axis_index("group"), lax.axis_index("member")
    core = lax.rem(me, CORES)
    y = lax.rem(lax.div(me, CORES), wide)
    z = lax.div(me, CORES * wide)
    gx, gy = lax.rem(g, along_x), lax.div(g, along_x)

    def member(zz, yy, cc):
        return (zz * wide + yy) * CORES + cc

    partner = (g, member(z, y, 1 - core))
    group_peers = {}
    for r in range(1, groups):
        dy, dx = r // along_x, r % along_x
        group_peers[r] = lax.rem(gy + dy, 2) * along_x + lax.rem(gx + dx, along_x)
    up = (g, member(lax.rem(z + 1, depth), y, core))
    down = (g, member(lax.rem(z + depth - 1, depth), y, core))
    y_peers = [lax.rem(y + r, wide) for r in range(1, wide)]

    def z_chunk(j):
        away = half_depth - j // 2 if j % 2 == 0 else half_depth + (j + 1) // 2
        return lax.rem(z + away, depth)

    load = pltpu.make_async_copy(points, rows_in, load_sem)
    load.start()
    table_loads = []
    for j in range(depth):
        table_loads.append(
            pltpu.make_async_copy(table.at[z_chunk(j), :, core], cents.at[j], table_sem.at[j])
        )
        table_loads[-1].start()

    barrier = pltpu.get_barrier_semaphore()
    greeted = [(group_peers[r], me) for r in range(1, groups)]
    greeted += [partner, up, down] + [(g, member(z, yy, core)) for yy in y_peers]
    for peer in greeted:
        pl.semaphore_signal(barrier, inc=1, device_id=peer, device_id_type=MESH)

    destination = dest[...]
    named = iota((16, count), 0) == destination
    earlier = (iota((count, count), 0) < iota((count, count), 1)).astype(F32).astype(BF16)
    before = jnp.dot(named.astype(F32).astype(BF16), earlier, preferred_element_type=F32)
    rank = jnp.sum(jnp.where(named, before, 0.0), axis=0, keepdims=True)
    slot = destination * capacity + rank.astype(I32)
    slots = groups * capacity
    place = (iota((slots, count), 0) == slot).astype(F32).astype(BF16)
    load.wait()
    moved = jnp.dot(place, rows_in[...], preferred_element_type=F32)
    used = jnp.dot(place, jnp.ones((count, 128), BF16), preferred_element_type=F32)
    mark = jnp.where((iota((slots, 128), 1) == 0) & (used < 0.5), UNUSED, 0.0)
    packed[:, :, :128] = (moved[:, :128] + mark).astype(BF16).reshape(groups, capacity, 128)
    packed[:, :, 128:] = moved[:, 128:].astype(BF16).reshape(groups, capacity, width - 128)

    pl.semaphore_wait(barrier, len(greeted))

    started = []

    def send(src, dst, send_sem, recv_sem, to):
        copy = pltpu.make_async_remote_copy(
            src_ref=src, dst_ref=dst, send_sem=send_sem, recv_sem=recv_sem,
            device_id=to, device_id_type=MESH,
        )
        copy.start()
        started.append(copy)
        return copy

    arrivals = {}
    for r in range(1, groups):
        arrivals[r] = send(
            packed.at[group_peers[r]], rows.at[0, r], a_send.at[r], a_recv.at[r],
            (group_peers[r], me),
        )
    forwards = [send(packed.at[g], rows.at[1, 0], f_send.at[0], f_recv.at[0], partner)]
    rows[0, 0] = packed[g]

    def forward(r):
        arrivals[r].wait_recv()
        forwards.append(
            send(rows.at[0, r], rows.at[1, r], f_send.at[r], f_recv.at[r], partner)
        )

    for j in range(depth):
        table_loads[j].wait()
    per = batch * chunk

    @pl.loop(0, depth // batch)
    def _(i):
        c = cents[pl.ds(i * batch, batch)].reshape(per, width).astype(F32)
        half_norms[pl.ds(i * per, per)] = 0.5 * jnp.sum(c * c, axis=1, keepdims=True)

    first = ((iota((16, width), 0) == 0) & (iota((16, width), 1) == 0)).astype(F32).astype(BF16)

    def score(b):
        half, quarter = divmod(b, 2)
        x = rows[half, quarter * along_x : (quarter + 1) * along_x].reshape(block, width)

        def raw(i, top):
            at = pl.ds(i * per, per)
            c = cents[pl.ds(i * batch, batch)].reshape(per, width)
            s = lax.dot_general(c, x, NT, preferred_element_type=F32)
            s = SCALE * (s - half_norms[at])
            scores[b, at] = s
            return jnp.maximum(top, jnp.max(s.reshape(per // 8, 8, block), axis=0))

        top = lax.fori_loop(0, depth // batch, raw, jnp.full((8, block), -jnp.inf, F32))
        top = jnp.max(top, axis=0, keepdims=True)

        def exps(i, low):
            at = pl.ds(i * per, per)
            e = jnp.exp(scores[b, at] - top)
            scores[b, at] = e
            return low + jnp.sum(e.reshape(per // 8, 8, block), axis=0)

        low = lax.fori_loop(0, depth // batch, exps, jnp.zeros((8, block), F32))
        low = jnp.sum(low, axis=0, keepdims=True)
        stats[b, 0] = jnp.broadcast_to(top, (8, block))
        stats[b, 1] = jnp.broadcast_to(low, (8, block))
        send(stats.at[b], other_stats.at[(b + 2) % 4], s_send.at[b], s_recv.at[(b + 2) % 4], partner)
        column = lax.dot_general(first, x, NT, preferred_element_type=F32)
        return top, low, column[:1] < 0.5 * UNUSED

    for r in range(1, along_x):
        forward(r)
    blocks = [score(0)]
    for r in range(along_x, groups):
        forward(r)
    blocks.append(score(1))
    for r in range(along_x):
        forwards[r].wait_recv()
    blocks.append(score(2))
    for r in range(along_x, groups):
        forwards[r].wait_recv()
    blocks.append(score(3))

    def share(b):
        top, low, valid = blocks[b]
        pltpu.make_async_remote_copy(
            src_ref=stats.at[b], dst_ref=other_stats.at[b], send_sem=s_send.at[b],
            recv_sem=s_recv.at[b], device_id=partner, device_id_type=MESH,
        ).wait_recv()
        their_top, their_low = other_stats[b, 0][:1], other_stats[b, 1][:1]
        highest = jnp.maximum(top, their_top)
        mine = jnp.exp(top - highest)
        whole = low * mine + their_low * jnp.exp(their_top - highest)
        return jnp.where(valid, mine / whole, 0.0)

    shares = [share(b) for b in range(4)]
    diagonal = iota((chunk, 128), 0) == iota((chunk, 128), 1)

    def weigh(i):
        at = slice(i * per, (i + 1) * per)
        seen = jnp.zeros((per, 128), F32)
        for b in range(4):
            w = (scores[b, at] * shares[b]).astype(BF16)
            weights[at, b * block : (b + 1) * block] = w
            wide_w = w.astype(F32)
            for k in range(0, block, 128):
                seen = seen + wide_w[:, k : k + 128]
        column = jnp.sum(seen, axis=1, keepdims=True)
        for k in range(batch):
            part = column[k * chunk : (k + 1) * chunk]
            line = jnp.sum(jnp.where(diagonal, part, 0.0), axis=0, keepdims=True)
            counts[i * batch + k] = jnp.broadcast_to(line, (8, 128))
        sums[at] = jnp.dot(
            weights[at], rows[...].reshape(2 * groups * capacity, width), preferred_element_type=F32
        )

    half = chunk // 2

    def from_ring(d, t, u):
        z_copies[d, t, u].wait_recv()
        return z_in[d, t, u].astype(F32)

    def count_from_ring(d, t):
        zc_copies[d, t].wait_recv()
        return zc_in[d, t]

    z_copies, zc_copies = {}, {}

    def ring(t):
        ways = [(0, up)] + ([(1, down)] if t < half_depth - 1 else [])
        for u in range(2):
            for d, to in ways:
                j = 2 * t + d
                v = sums[j * chunk + u * half : j * chunk + (u + 1) * half]
                if t > 0:
                    v = v + from_ring(d, t - 1, u)
                z_out[d, t, u] = v.astype(BF16)
                z_copies[d, t, u] = send(
                    z_out.at[d, t, u], z_in.at[d, t, u], z_send.at[d, t, u], z_recv.at[d, t, u], to
                )
        for d, to in ways:
            v = counts[2 * t + d]
            if t > 0:
                v = v + count_from_ring(d, t - 1)
            zc_out[d, t] = v
            zc_copies[d, t] = send(
                zc_out.at[d, t], zc_in.at[d, t], zc_send.at[d, t], zc_recv.at[d, t], to
            )

    weigh(0)
    made = 1
    for t in range(half_depth):
        while made <= (2 * t + 1) // batch:
            weigh(made)
            made += 1
        ring(t)
        if made < depth // batch:
            weigh(made)
            made += 1
    while made < depth // batch:
        weigh(made)
        made += 1

    own = (depth - 1) * chunk
    for u in range(2):
        v = sums[own + u * half : own + (u + 1) * half]
        v = v + from_ring(0, half_depth - 1, u)
        if half_depth > 1:
            v = v + from_ring(1, half_depth - 2, u)
        pieces = half // piece
        total[u * pieces : (u + 1) * pieces] = v.reshape(pieces, piece, width)
        y_out[u * pieces : (u + 1) * pieces] = v.astype(BF16).reshape(pieces, piece, width)
    seen = counts[depth - 1] + count_from_ring(0, half_depth - 1)
    if half_depth > 1:
        seen = seen + count_from_ring(1, half_depth - 2)
    yc_out[...] = seen

    y_copies = []
    for k, yy in enumerate(y_peers):
        to = (g, member(z, yy, core))
        y_copies.append(
            (
                send(y_out.at[yy], y_in.at[k], y_send.at[k], y_recv.at[k], to),
                send(yc_out, yc_in.at[k], yc_send.at[k], yc_recv.at[k], to),
            )
        )
    new = total[y]
    for k, (copy, count_copy) in enumerate(y_copies):
        copy.wait_recv()
        new = new + y_in[k].astype(F32)
        count_copy.wait_recv()
        seen = seen + yc_in[k]
    pick = iota((piece, 128), 1) == iota((piece, 128), 0) + y * piece
    soft_count = jnp.sum(
        jnp.where(pick, jnp.broadcast_to(seen[:1], (piece, 128)), 0.0), axis=1, keepdims=True
    )
    old = cents[depth - 1, y].astype(F32)
    out[...] = ((new + old) / (soft_count + 1.0)).astype(BF16)

    for copy in started:
        copy.wait_send()


def build(mesh, wide, batch):
    groups, members = mesh.shape["group"], mesh.shape["member"]
    depth = members // (CORES * wide)

    def local(points, centroids, dest_group):
        count, width = points.shape
        fine = centroids.shape[0]
        piece = fine // members
        capacity = count // 4 if groups >= 4 else count // groups
        chunk = wide * piece
        half_fine = depth * chunk
        block = groups // 2 * capacity
        steps = depth // 2
        dma = pltpu.SemaphoreType.DMA
        vmem = pltpu.VMEM
        scratch = [
            vmem((count, width), BF16),
            vmem((groups, capacity, width), BF16),
            vmem((2, groups, capacity, width), BF16),
            vmem((depth, wide, piece, width), BF16),
            vmem((half_fine, 1), F32),
            vmem((4, half_fine, block), F32),
            vmem((half_fine, 4 * block), BF16),
            vmem((half_fine, width), F32),
            vmem((depth, 8, 128), F32),
            vmem((4, 2, 8, block), F32),
            vmem((4, 2, 8, block), F32),
            vmem((2, steps, 2, chunk // 2, width), BF16),
            vmem((2, steps, 2, chunk // 2, width), BF16),
            vmem((2, steps, 8, 128), F32),
            vmem((2, steps, 8, 128), F32),
            vmem((wide, piece, width), F32),
            vmem((wide, piece, width), BF16),
            vmem((wide - 1, piece, width), BF16),
            vmem((8, 128), F32),
            vmem((wide - 1, 8, 128), F32),
            dma,
            dma((depth,)),
            dma((groups,)), dma((groups,)), dma((groups,)), dma((groups,)),
            dma((4,)), dma((4,)),
            dma((2, steps, 2)), dma((2, steps, 2)), dma((2, steps)), dma((2, steps)),
            dma((wide - 1,)), dma((wide - 1,)), dma((wide - 1,)), dma((wide - 1,)),
        ]
        table = centroids.reshape(depth, wide, CORES, piece, width)
        return pl.pallas_call(
            functools.partial(refit, groups, depth, wide, batch),
            out_shape=jax.ShapeDtypeStruct((piece, width), BF16),
            in_specs=[
                pl.BlockSpec(memory_space=pl.ANY),
                pl.BlockSpec(memory_space=pl.ANY),
                pl.BlockSpec(memory_space=pltpu.VMEM),
            ],
            out_specs=pl.BlockSpec(memory_space=pltpu.VMEM),
            scratch_shapes=scratch,
            compiler_params=pltpu.CompilerParams(collective_id=0, has_side_effects=True),
            name="refit",
        )(points, table, dest_group.reshape(1, count))

    both = P(("group", "member"), None)
    return jax.shard_map(
        local, mesh=mesh, in_specs=(both, P("group", None), both), out_specs=both, check_vma=False
    )


def solution(mesh):
    return build(mesh, HIGH_Y, 4)
```

time: 269 us -> 77.2 us (0.29)
  the two profiles are of different devices: /device:TPU:4 before, /device:TPU:8 now
where the time goes in v1:
time: 77.2 us; the launch traced here: 77 us
  Pallas kernels  75.6 us (98%)
  local copies, waits for them, and re-layouts  1.35 us (2%)
    pallas_call x1, Pallas kernels, local(): pl.pallas_call(functools.partial(refit, groups, depth, wide, batch), out_...  75.6 us

profile of v1, /device:TPU:8, one launch (start us, length us, event | category | flops | bytes accessed | tf_op | source)
XLA Modules:
  0.0 77.0 jit_solution(13840170457036469770)
XLA Ops:
  0.0 75.6 %refit.1 = bf16[16,768]{1,0:T(8,128)(2,1)} custom-call(bf16[256,768]{1,0:T(8,128)(2,1)} %points.1, bf16[16,4,2,16,768]{4,3,2,1,0:T(8,128)(2,1)} %bitcast.2, s32[1,256]{1,0:T(1,128)} %bitcast.3), custom_call_target="tpu_custom_call" | custom-call | tf_op jit(solution)/shard_map/refit/pallas_call | solution.py:336
  75.6 1.3 %copy.5 = bf16[16,768]{1,0:T(8,128)(2,1)} copy(bf16[16,768]{1,0:T(8,128)(2,1)} %refit.1) | data formatting | bytes 49152
